TPU v7x, 128 devices: a whole 4x4x4 slice. The times are simulated.
128 devices in a mesh: grp: 2 (over z_hi), pix: 64 (over x, y, z_lo, core).
Axes of the slice: x: 4, y: 4, z: 4 (z_hi: 2, z_lo: 2; z = z_hi * 2 + z_lo), core: 2. Of those that a mesh axis runs over, the one named last changes fastest.
Arguments:
- fields: bfloat16 [2, 2, 128, 512, 512], P('grp', None, None, 'pix'), may hold values from -6 to 6
- lens_phase: float32 [512, 512], P('pix'), may hold values from -3.140625 to 3.140625
- occupancy: float32 [256], replicated, may hold values from 0.05 to 1
- focus_scale: float32 [256], replicated, may hold values from 0.5 to 1.5
- assignment: int32 [256], replicated, may hold values from 0 to 255, each once
- start_basis: float32 [2, 256, 128], replicated, may hold values from -6 to 6
Outputs:
- coherent_modes: bfloat16 [2, 128, 512, 512], P(None, None, 'pix', 'grp')
- relative_power: float32 [128], replicated
Inputs may be any that keep to these rules, and one draw needn't show every extreme that they name: `assignment`: each electron is carried by exactly one wavefront slot.
All inputs are finite; a program needn't handle non-finite values.
Results may differ from a plain program's by a relative error of at most 0.0018.
The roundings to bfloat16 on the way count: a program that leaves them out, or rounds other values in their place, can miss the bound.
Values may be sent and summed in bfloat16 or wider, within the bound.
No kernel may reach another device: no remote copies, remote signals or barrier semaphores. Data moves between devices by JAX's collectives and lax.ppermute only.
A program may use at most 64 MiB of HBM per device.

v0:
```python
import math

import jax
import jax.numpy as jnp
from jax import lax
from jax.sharding import PartitionSpec as P

NROW = 512
NCOL = 512
STEPS = 2


def partner_2(array, axis, apart):
    return lax.ppermute(array, axis, [(i, i ^ 1 << apart) for i in range(lax.axis_size(axis))])


def dft_tables(length):
    index = jnp.arange(length, dtype=jnp.int32)
    product = index[:, None] * index[None, :] % length
    angle = product.astype(jnp.float32) * (2.0 * math.pi / length)
    factor = 1.0 / math.sqrt(length)
    return (
        (jnp.cos(angle) * factor).astype(jnp.bfloat16),
        (jnp.sin(angle) * factor).astype(jnp.bfloat16),
    )


def local(fields, lens_phase, occupancy, focus_scale, assignment, start_basis):
    highest = lax.Precision.HIGHEST
    local_fields = fields[0]
    modes = local_fields.shape[1]
    group_index = lax.axis_index("grp")
    electron = lax.dynamic_slice_in_dim(assignment, group_index * modes, modes)
    choose = (
        electron[:, None] == jnp.arange(assignment.shape[0], dtype=jnp.int32)[None, :]
    ).astype(jnp.float32)
    amplitude = jnp.sqrt(jnp.sum(choose * occupancy[None, :], axis=1))[:, None, None]
    chromatic = jnp.sum(choose * focus_scale[None, :], axis=1)
    angle = chromatic[:, None, None] * lens_phase[None]
    cosine = jnp.cos(angle)
    sine = jnp.sin(angle)
    field_re = local_fields[0].astype(jnp.float32)
    field_im = local_fields[1].astype(jnp.float32)
    phased = jnp.stack(
        [
            amplitude * (field_re * cosine - field_im * sine),
            amplitude * (field_re * sine + field_im * cosine),
        ]
    ).astype(jnp.bfloat16)
    cos_cols, sin_cols = dft_tables(lens_phase.shape[1])
    col_cos = jnp.einsum("zmrc,ck->zmkr", phased, cos_cols, preferred_element_type=jnp.float32)
    col_sin = jnp.einsum("zmrc,ck->zmkr", phased, sin_cols, preferred_element_type=jnp.float32)
    across = jnp.stack([col_cos[0] + col_sin[1], col_cos[1] - col_sin[0]]).astype(jnp.bfloat16)
    full_rows = across.shape[3] * lax.axis_size("pix")
    cos_rows, sin_rows = dft_tables(full_rows)
    pieces = lax.all_to_all(across, "pix", split_axis=2, concat_axis=3, tiled=True)
    row_cos = jnp.dot(pieces, cos_rows, preferred_element_type=jnp.float32)
    row_sin = jnp.dot(pieces, sin_rows, preferred_element_type=jnp.float32)
    focal = jnp.stack([row_cos[0] + row_sin[1], row_cos[1] - row_sin[0]]).astype(jnp.bfloat16)
    stack_size = modes * lax.axis_size("grp")
    half_rows = full_rows // lax.axis_size("grp")
    partner = partner_2(focal, "grp", 0)
    leading = jnp.where(group_index == 0, focal, partner)
    trailing = jnp.where(group_index == 0, partner, focal)
    stacked = jnp.concatenate([leading, trailing], axis=1)
    flat = stacked.reshape(2, stack_size, -1)
    blocks = jnp.einsum("xap,ybp->xyab", flat, flat, preferred_element_type=jnp.float32)
    local_re = blocks[0, 0] + blocks[1, 1]
    local_im = blocks[0, 1] - blocks[1, 0]
    gram_re, gram_im = lax.psum((local_re, local_im), "pix")
    owned = lax.dynamic_slice_in_dim(stacked, group_index * half_rows, half_rows, 3)
    basis_re = start_basis[0]
    basis_im = start_basis[1]
    for iteration in range(STEPS):
        image_re = jnp.dot(gram_re, basis_re, precision=highest) - jnp.dot(
            gram_im, basis_im, precision=highest
        )
        image_im = jnp.dot(gram_re, basis_im, precision=highest) + jnp.dot(
            gram_im, basis_re, precision=highest
        )
        column_norm = jnp.sqrt(jnp.sum(image_re * image_re + image_im * image_im, axis=0) + 1e-06)
        basis_re = image_re / column_norm[None, :]
        basis_im = image_im / column_norm[None, :]
    rounded = jnp.stack([basis_re, basis_im]).astype(jnp.bfloat16)
    rank = rounded.shape[2]
    owned_flat = owned.reshape(2, stack_size, -1)
    products = jnp.einsum("xsk,ysp->xykp", rounded, owned_flat, preferred_element_type=jnp.float32)
    mode_re = products[0, 0] - products[1, 1]
    mode_im = products[0, 1] + products[1, 0]
    energy = lax.psum(jnp.sum(mode_re * mode_re + mode_im * mode_im, axis=1), ("grp", "pix"))
    trace = jnp.sum(jnp.diagonal(gram_re))
    relative_power = energy * stack_size / trace
    inverse = lax.rsqrt(energy / (NROW * NCOL) + 1e-06)
    coherent_modes = (jnp.stack([mode_re, mode_im]) * inverse[None, :, None]).astype(jnp.bfloat16)
    return (coherent_modes.reshape(2, rank, owned.shape[2], owned.shape[3]), relative_power)


def solution(mesh):
    in_specs = (P("grp", None, None, "pix", None), P("pix", None), P(), P(), P(), P())
    out_specs = (P(None, None, "pix", "grp"), P())
    return jax.shard_map(local, mesh=mesh, in_specs=in_specs, out_specs=out_specs, check_vma=False)
```

profile of v0, /device:TPU:1, one launch (start us, length us, event | category | flops | bytes accessed | tf_op | source)
XLA Modules:
  0.0 779.3 jit_solution(8011462047435173882)
XLA Ops:
  7.2 0.8 dynamic_slice.6
  8.0 0.9 select_reduce_fusion.1
  8.9 1.7 fusion.84
  10.6 8.9 %fusion.9 = (bf16[1,128,8,512]{3,1,2,0:T(8,128)(2,1)S(1)}, bf16[1,128,8,512]{3,1,2,0:T(8,128)(2,1)S(1)}) fusion(f32[8,512]{1,0:T(8,128)S(1)} %copy-done.5, f32[128]{0:T(128)S(1)} %get-tuple-element.3, f32[128]{0:T(128)S(1)} %sqrt.21, bf16[1,1,128,8,512]{4,3,2,1,0:T(8,128)(2,1)S(1)} %get-tuple-element.18, bf16[1,1,128,8,512]{4,3,2,1,0:T(8,128)(2,1)S(1)} %get-tuple-element.17), kind=kLoop, calls=%fused_computation.18 | loop fusion | flops 6815744 | bytes 4211712 | tf_op jit(solution)/shard_map/convert.10
  19.5 4.9 convolution_bitcast_fusion.2
  24.4 5.0 convolution_bitcast_fusion.1
  30.1 1.6 copy.51
  31.6 39.1 %all_to_all.18 = bf16[2,128,512,8]{1,3,0,2:T(8,128)(2,1)S(1)} all-to-all(bf16[2,128,512,8]{1,3,0,2:T(8,128)(2,1)S(1)} %copy.51), channel_id=1, replica_groups=mesh['grp'=2,'pix'=64] {'pix'}, dimensions={2} | all-to-all | bytes 4194304 | tf_op jit(solution)/shard_map/all_to_all | solution.py:56
  70.8 4.8 fusion.19
  75.6 4.8 fusion.21
  80.3 1.3 fusion.15
  81.6 1.5 pad_maximum_fusion.4
  83.1 3.6 collective-permute-start
  86.7 46.2 %collective-permute-done = bf16[2,128,8,512]{3,1,2,0:T(8,128)(2,1)} collective-permute-done((bf16[2,128,8,512]{3,1,2,0:T(8,128)(2,1)}, bf16[2,128,8,512]{3,1,2,0:T(8,128)(2,1)}, u32[]{:S(2)}, u32[]{:S(2)}) %collective-permute-start) | collective-permute-done | bytes 2097184 | tf_op jit(solution)/shard_map/ppermute | solution.py:14
  133.0 1.9 broadcast_select_fusion
  134.8 2.4 fusion.25
  137.2 0.9 fusion.42
  138.1 3.1 fusion.13
  141.3 2.9 copy.56
  144.2 544.8 %all-reduce.3.cloned.1.call-done = (f32[256,256]{0,1:T(8,128)}, f32[256,256]{0,1:T(8,128)}) async-done(((f32[256,256]{0,1:T(8,128)}, f32[256,256]{0,1:T(8,128)}), (f32[256,256]{0,1:T(8,128)}, f32[256,256]{0,1:T(8,128)})) %all-reduce.3.cloned.1.call-update) | async-done | bytes 524304 | tf_op jit(solution)/shard_map/psum | solution.py:70
  688.9 1.6 fusion.50
  690.6 1.5 fusion.46
  692.1 1.5 convolution_subtract_fusion.1
  693.6 1.6 add_reduce_fusion.2
  696.4 0.6 convolution_subtract_fusion
  697.0 0.6 add_reduce_fusion.1
  697.7 0.7 convolution_bitcast_fusion
  698.7 67.0 %psum.23 = f32[128]{0:T(128)S(1)} all-reduce(f32[128]{0:T(128)S(1)} %get-tuple-element.6), channel_id=1, replica_groups=mesh['grp'=2,'pix'=64] {'grp','pix'}, use_global_device_ids=true, to_apply=%region_7.8 | all-reduce | flops 128 | bytes 1024 | tf_op jit(solution)/shard_map/psum | solution.py:90
  765.8 2.4 gather_fusion
  769.1 0.6 reduce_sum.59
  769.7 1.2 multiply_divide_fusion
  770.9 1.2 fusion.18
  (26 shorter events, 3.3 us)
Async XLA Ops:
  7.2 681.8 %all-reduce.3.cloned.1.call-start = ((), (), s32[]{:S(2)}) async-start(), calls=%async_computation.1 | async-start | bytes 1048576 | tf_op jit(solution)/shard_map/psum | solution.py:70
  8.9 1.7 copy-start.5
  83.1 49.8 %collective-permute-start = (bf16[2,128,8,512]{3,1,2,0:T(8,128)(2,1)}, bf16[2,128,8,512]{3,1,2,0:T(8,128)(2,1)}, u32[]{:S(2)}, u32[]{:S(2)}) collective-permute-start(bf16[2,128,8,512]{3,1,2,0:T(8,128)(2,1)} %pad_maximum_fusion.4), channel_id=1, source_target_pairs={{0,64},{64,0},{1,65},{65,1},{2,66},{66,2},{3,67},{67,3},{4,68},{68... | collective-permute-start | bytes 6291464 | tf_op jit(solution)/shard_map/ppermute | solution.py:14
  134.8 2.4 copy-start.1
  134.8 2.4 copy-start.2
  141.3 547.7 %copy-start.4 = (f32[2,256,128]{2,1,0:T(8,128)S(1)}, f32[2,256,128]{2,1,0:T(8,128)}, u32[]{:S(2)}) copy-start(f32[2,256,128]{2,1,0:T(8,128)} %param.11) | copy-start | bytes 786436
  688.9 6.3 copy-start
  688.9 7.5 copy-start.3
Sparse Core Ops, SparseCore 0:
  138.2 550.6 all-reduce.2
where the time goes:
time: 782 us; the launch traced here: 779 us
  waiting for transfers between devices  591 us (76%)
  blocking collectives  106 us (14%)
  matrix products  31.2 us (4%)
  other arithmetic  22.4 us (3%)
  between operations  14.7 us (2%)
  local copies, waits for them, and re-layouts  10.2 us (1%)
    psum x1, waiting for transfers between devices, local(): gram_re, gram_im = lax.psum((local_re, local_im), 'pix')  545 us
    psum x1, blocking collectives, local(): lax.psum(jnp.sum(mode_re * mode_re + mode_im * mode_im, axis=1), ('grp',...  67 us
    ppermute x1, waiting for transfers between devices, partner_2(): lax.ppermute(array, axis, [(i, i ^ 1 << apart) for i in range(lax.axis_si...  46.2 us
    all_to_all x1, blocking collectives, local(): lax.all_to_all(across, 'pix', split_axis=2, concat_axis=3, tiled=True)  39.1 us
  transfers between devices with their start and end apart: 2, of which 2 were waited for; matrix products, arithmetic and copies ran while one was open for 1% of the time, Pallas kernels for 0%

commit v1 on v0

v1 whole, which is shorter than its diff:
```python
import math

import jax
import jax.numpy as jnp
import numpy as np
from jax import lax
from jax.experimental import pallas as pl
from jax.experimental.pallas import tpu as pltpu
from jax.sharding import PartitionSpec as P

NROW = 512
NCOL = 512
STEPS = 2
GROUPS = 2
PIX = 64
DEVICES = GROUPS * PIX
SLOTS = 128
STACK = GROUPS * SLOTS
RANK = 128
ROWS = NROW // PIX
COLS = NCOL // DEVICES
HALF = NROW // GROUPS
WIDE = RANK * GROUPS * COLS
AXES = ("grp", "pix")

PI_HI = 3.140625
PI_LO = math.pi - 3.140625


def fit(function, terms):
    limit = (math.pi / 2) * 1.001
    nodes = np.cos(np.pi * (np.arange(400) + 0.5) / 400)
    square = (nodes + 1.0) * 0.5 * limit * limit
    powers = np.stack([square**k for k in range(terms)], axis=1)
    return [float(c) for c in np.linalg.lstsq(powers, function(np.sqrt(square)), rcond=None)[0]]


SIN_FIT = fit(lambda x: np.sin(x) / x, 5)
COS_FIT = fit(np.cos, 6)


def tables(length):
    index = np.arange(length, dtype=np.int64)
    angle = (index[:, None] * index[None, :] % length).astype(np.float32) * np.float32(
        2.0 * math.pi / length
    )
    factor = np.float32(1.0 / math.sqrt(length))
    cosine = (np.cos(angle) * factor).astype(jnp.bfloat16)
    sine = (np.sin(angle) * factor).astype(jnp.bfloat16)
    return cosine, sine


def column_tables():
    i, g, p = np.meshgrid(np.arange(COLS), np.arange(GROUPS), np.arange(PIX), indexing="ij")
    order = (p * (GROUPS * COLS) + g * COLS + i).reshape(-1)
    cosine, sine = tables(NCOL)
    return cosine[order], sine[order]


def row_tables():
    cosine, sine = tables(NROW)
    cosine = cosine.reshape(NROW, PIX, ROWS)
    sine = sine.reshape(NROW, PIX, ROWS)
    real = np.stack([cosine, sine], axis=2).reshape(NROW, 2 * NROW)
    imag = np.stack([-sine, cosine], axis=2).reshape(NROW, 2 * NROW)
    return np.concatenate([real, imag], axis=0)


def polynomial(square, coefficients):
    total = square * coefficients[-1] + coefficients[-2]
    for coefficient in coefficients[-3::-1]:
        total = total * square + coefficient
    return total


def spectra_kernel(
    group_ref, assign_ref, occ_ref, chrom_ref, fields_ref, lens_ref, cos_ref, sin_ref, out_ref,
    real_ref, imag_ref, wide_ref,
):
    base = group_ref[0] * SLOTS

    def phase(m, carry):
        electron = assign_ref[base + m]
        amplitude = jnp.sqrt(jnp.full((ROWS, 128), occ_ref[electron], jnp.float32))
        chromatic = chrom_ref[electron]
        for lane in range(NCOL // 128):
            cut = pl.ds(lane * 128, 128)
            angle = lens_ref[:, cut] * chromatic
            turns = jnp.round(angle * (1.0 / math.pi))
            rest = (angle - turns * PI_HI) - turns * PI_LO
            square = rest * rest
            signed = amplitude * (1.0 - 2.0 * (turns * turns))
            sine = signed * (rest * polynomial(square, SIN_FIT))
            cosine = signed * polynomial(square, COS_FIT)
            field_re = fields_ref[0, m, :, cut].astype(jnp.float32)
            field_im = fields_ref[1, m, :, cut].astype(jnp.float32)
            rows = pl.ds(lane * ROWS * SLOTS + m, ROWS, stride=SLOTS)
            real_ref[rows, :] = field_re * cosine - field_im * sine
            imag_ref[rows, :] = field_re * sine + field_im * cosine
        return carry

    lax.fori_loop(0, SLOTS, phase, 0, unroll=2)
    contract = (((1,), (1,)), ((), ()))

    def product(table, wave):
        return lax.dot_general(table, wave, contract, preferred_element_type=jnp.float32)

    def wave(ref, j):
        lanes = [
            ref[pl.ds((lane * ROWS + j) * SLOTS, 2 * SLOTS), :] for lane in range(NCOL // 128)
        ]
        return jnp.concatenate(lanes, axis=1).astype(jnp.bfloat16)

    def spectrum(i, carry):
        rows = pl.ds(pl.multiple_of(i * DEVICES, DEVICES), DEVICES)
        cosine = cos_ref[rows, :]
        sine = sin_ref[rows, :]
        for j in range(0, ROWS, 2):
            wave_re = wave(real_ref, j)
            wave_im = wave(imag_ref, j)
            across_re = product(cosine, wave_re) + product(sine, wave_im)
            across_im = product(cosine, wave_im) - product(sine, wave_re)
            for part, across in ((0, across_re), (1, across_im)):
                for q in range(2):
                    at = part * ROWS + j + q
                    wide_ref[pl.ds(at, DEVICES, stride=2 * ROWS), :] = across[
                        :, q * SLOTS : (q + 1) * SLOTS
                    ]
        out_ref[:, i] = wide_ref[...].astype(jnp.bfloat16).reshape(DEVICES, 2 * ROWS, SLOTS)
        return carry

    lax.fori_loop(0, COLS, spectrum, 0)


def focal_kernel(group_ref, pieces_ref, table_ref, keep_ref, send_ref, gram_ref):
    group = group_ref[0]
    real = jnp.zeros((STACK, STACK), jnp.float32)
    cross = jnp.zeros((STACK, STACK), jnp.float32)
    for i in range(COLS):
        wave = jnp.concatenate(
            [
                pieces_ref[g * PIX : (g + 1) * PIX, i].reshape(2 * NROW, SLOTS)
                for g in range(GROUPS)
            ],
            axis=1,
        )
        focal = [
            jnp.dot(
                table_ref[part * NROW : (part + 1) * NROW, :],
                wave,
                preferred_element_type=jnp.float32,
            ).astype(jnp.bfloat16)
            for part in range(2)
        ]
        turned = [focal[part].T for part in range(2)]
        for part in range(2):
            low, high = turned[part][:, :HALF], turned[part][:, HALF:]
            keep_ref[part, i] = jnp.where(group == 0, low, high)
            send_ref[part, i] = jnp.where(group == 0, high, low)
        real += jnp.dot(turned[0], focal[0], preferred_element_type=jnp.float32)
        real += jnp.dot(turned[1], focal[1], preferred_element_type=jnp.float32)
        cross += jnp.dot(turned[0], focal[1], preferred_element_type=jnp.float32)
    imag = cross - cross.T
    row = lax.broadcasted_iota(jnp.int32, (STACK, STACK), 0)
    column = lax.broadcasted_iota(jnp.int32, (STACK, STACK), 1)
    packed = jnp.where(row <= column, real, imag)
    for q in range(4):
        top, left = (q // 2) * 128, (q % 2) * 128
        gram_ref[pl.ds(q, 128, stride=4), :] = packed[top : top + 128, left : left + 128]


def total_kernel(parts_ref, out_ref):
    total = jnp.sum(parts_ref[...].reshape(DEVICES // 2, 8, 128), axis=0)
    total = total[:4] + total[4:]
    twice = jnp.concatenate([total, total], axis=0)
    out_ref[...] = jnp.broadcast_to(twice[None], (DEVICES // 2, 8, 128)).reshape(4 * DEVICES, 128)


def modes_kernel(group_ref, gram_ref, start_ref, keep_ref, other_ref, out_ref, power_ref, wide_ref):
    highest = lax.Precision.HIGHEST
    quads = [gram_ref[pl.ds(q, 128, stride=4), :] for q in range(4)]
    packed = jnp.concatenate(
        [jnp.concatenate(quads[:2], axis=1), jnp.concatenate(quads[2:], axis=1)], axis=0
    )
    turned = packed.T
    row = lax.broadcasted_iota(jnp.int32, (STACK, STACK), 0)
    column = lax.broadcasted_iota(jnp.int32, (STACK, STACK), 1)
    gram_re = jnp.where(row <= column, packed, turned)
    gram_im = jnp.where(row > column, packed, jnp.where(row == column, 0.0, -turned))

    def product(a, b):
        return jnp.dot(a, b, precision=highest, preferred_element_type=jnp.float32)

    def apply(re, im):
        return (
            product(gram_re, re) - product(gram_im, im),
            product(gram_re, im) + product(gram_im, re),
        )

    basis_re, basis_im = start_ref[0], start_ref[1]
    for _ in range(STEPS):
        image_re, image_im = apply(basis_re, basis_im)
        norm = jnp.sqrt(
            jnp.sum(image_re * image_re + image_im * image_im, axis=0, keepdims=True) + 1e-06
        )
        basis_re = image_re / norm
        basis_im = image_im / norm
    rounded_re = basis_re.astype(jnp.bfloat16)
    rounded_im = basis_im.astype(jnp.bfloat16)
    wide_re = rounded_re.astype(jnp.float32)
    wide_im = rounded_im.astype(jnp.float32)
    image_re, image_im = apply(wide_re, wide_im)
    energy = jnp.sum(wide_re * image_re + wide_im * image_im, axis=0, keepdims=True)
    trace = jnp.sum(jnp.where(row == column, packed, 0.0))
    power_ref[...] = energy * STACK / trace
    inverse = lax.rsqrt(energy / (NROW * NCOL) + 1e-06)
    scale = jnp.broadcast_to(inverse, (RANK, RANK)).T
    left_re = wide_re.T.astype(jnp.bfloat16)
    left_im = wide_im.T.astype(jnp.bfloat16)
    group = group_ref[0]

    def multiply(a, b):
        return jnp.dot(a, b, preferred_element_type=jnp.float32)

    for part in range(2):
        for source, ref in ((0, keep_ref), (1, other_ref)):
            first = jnp.where(group == source, 0, COLS)
            for i in range(COLS):
                focal_re, focal_im = ref[0, i], ref[1, i]
                if part == 0:
                    mode = multiply(left_re, focal_re) - multiply(left_im, focal_im)
                else:
                    mode = multiply(left_re, focal_im) + multiply(left_im, focal_re)
                for lane in range(HALF // 128):
                    rows = pl.ds(lane * WIDE + first + i, RANK, stride=GROUPS * COLS)
                    wide_ref[rows, :] = mode[:, lane * 128 : (lane + 1) * 128] * scale
        for lane in range(HALF // 128):
            out_ref[part, :, :, lane * 128 : (lane + 1) * 128] = (
                wide_ref[lane * WIDE : (lane + 1) * WIDE, :]
                .reshape(RANK, GROUPS * COLS, 128)
                .astype(jnp.bfloat16)
            )


VMEM = pl.BlockSpec(memory_space=pltpu.VMEM)
SMEM = pl.BlockSpec(memory_space=pltpu.SMEM)
PARAMS = pltpu.CompilerParams(vmem_limit_bytes=56 * 1024 * 1024)


def local(fields, lens_phase, occupancy, focus_scale, assignment, start_basis):
    group = lax.axis_index("grp").astype(jnp.int32).reshape(1)
    cos_cols, sin_cols = (jnp.asarray(table) for table in column_tables())
    across = pl.pallas_call(
        spectra_kernel,
        out_shape=jax.ShapeDtypeStruct((DEVICES, COLS, 2 * ROWS, SLOTS), jnp.bfloat16),
        in_specs=[SMEM] * 4 + [VMEM] * 4,
        out_specs=VMEM,
        scratch_shapes=[
            pltpu.VMEM((NCOL // 128 * ROWS * SLOTS, 128), jnp.float32),
            pltpu.VMEM((NCOL // 128 * ROWS * SLOTS, 128), jnp.float32),
            pltpu.VMEM((DEVICES * 2 * ROWS, SLOTS), jnp.float32),
        ],
        compiler_params=PARAMS,
        name="spectra",
    )(group, assignment, occupancy, focus_scale, fields[0], lens_phase, cos_cols, sin_cols)
    pieces = lax.all_to_all(across, AXES, 0, 0, tiled=True)
    focal_shape = jax.ShapeDtypeStruct((2, COLS, STACK, HALF), jnp.bfloat16)
    keep, send, gram = pl.pallas_call(
        focal_kernel,
        out_shape=(
            focal_shape,
            focal_shape,
            jax.ShapeDtypeStruct((4 * DEVICES, 128), jnp.float32),
        ),
        in_specs=[SMEM] + [VMEM] * 2,
        out_specs=(VMEM,) * 3,
        compiler_params=PARAMS,
        name="focal",
    )(group, pieces, jnp.asarray(row_tables()))
    other = lax.ppermute(send, "grp", [(0, 1), (1, 0)])
    parts = lax.all_to_all(gram.reshape(DEVICES, 4, 128), AXES, 0, 0, tiled=True)
    total = pl.pallas_call(
        total_kernel,
        out_shape=jax.ShapeDtypeStruct((4 * DEVICES, 128), jnp.float32),
        in_specs=[VMEM],
        out_specs=VMEM,
        compiler_params=PARAMS,
        name="total",
    )(parts.reshape(4 * DEVICES, 128))
    whole = lax.all_to_all(total.reshape(DEVICES, 4, 128), AXES, 0, 0, tiled=True)
    coherent_modes, power = pl.pallas_call(
        modes_kernel,
        out_shape=(
            jax.ShapeDtypeStruct((2, RANK, GROUPS * COLS, HALF), jnp.bfloat16),
            jax.ShapeDtypeStruct((1, RANK), jnp.float32),
        ),
        in_specs=[SMEM] + [VMEM] * 4,
        out_specs=(VMEM,) * 2,
        scratch_shapes=[pltpu.VMEM((HALF // 128 * WIDE, 128), jnp.float32)],
        compiler_params=PARAMS,
        name="modes",
    )(group, whole.reshape(4 * DEVICES, 128), start_basis, keep, other)
    return coherent_modes, power.reshape(RANK)


def solution(mesh):
    in_specs = (P("grp", None, None, "pix", None), P("pix", None), P(), P(), P(), P())
    out_specs = (P(None, None, "pix", "grp"), P())
    return jax.shard_map(local, mesh=mesh, in_specs=in_specs, out_specs=out_specs, check_vma=False)
```

time: 782 us -> 122 us (0.16)
  waiting for transfers between devices: 591 us -> 0.01 us
  Pallas kernels: 0 us -> 33.1 us
  matrix products: 31.2 us -> 0 us
  other arithmetic: 22.4 us -> 0 us
  blocking collectives: 106 us -> 86.3 us
  between operations: 14.7 us -> 0.64 us
  local copies, waits for them, and re-layouts: 10.2 us -> 0.97 us
    psum x1 -> x0, waiting for transfers between devices: 545 us -> none  [local(): gram_re, gram_im = lax.psum((local_re, local_im), 'pix')]
    psum x1 -> x0, blocking collectives: 67 us -> none  [local(): lax.psum(jnp.sum(mode_re * mode_re + mode_im * mode_im, axis=1), ('grp',...]
    all_to_all x1 -> x3, blocking collectives: 39.1 us -> 86.3 us  [the longest x1 41.7 us: local(): pieces = lax.all_to_all(across, AXES, 0, 0, tiled=True)]
    ppermute x1, waiting for transfers between devices: 46.2 us -> 0.01 us  [local(): other = lax.ppermute(send, 'grp', [(0, 1), (1, 0)])]
    pallas_call x0 -> x4, Pallas kernels: none -> 33.1 us  [the longest x1 16.6 us: local(): pl.pallas_call(spectra_kernel, out_shape=jax.ShapeDtypeStruct((DEVICES, C...]
    dot_general x14 -> x0, matrix products: 31.2 us -> none  [the longest x1 4.97 us: local(): jnp.einsum('zmrc,ck->zmkr', phased, sin_cols, preferred_element_type=jnp....]
    another operation x6 -> x0, other arithmetic: 12.4 us -> none
  transfers between devices with their start and end apart: 2 -> 1, of which waited for: 2 -> 0; matrix products, arithmetic and copies ran while one was open for 1% -> 0% of each run, Pallas kernels for 0% -> 1%
where the time goes in v1:
time: 122 us
  blocking collectives  86.3 us (71%)
  Pallas kernels  33.1 us (27%)
    all_to_all x1, blocking collectives, local(): pieces = lax.all_to_all(across, AXES, 0, 0, tiled=True)  41.7 us
    all_to_all x1, blocking collectives, local(): lax.all_to_all(gram.reshape(DEVICES, 4, 128), AXES, 0, 0, tiled=True)  28.7 us
    pallas_call x1, Pallas kernels, local(): pl.pallas_call(spectra_kernel, out_shape=jax.ShapeDtypeStruct((DEVICES, C...  16.6 us
    all_to_all x1, blocking collectives, local(): lax.all_to_all(total.reshape(DEVICES, 4, 128), AXES, 0, 0, tiled=True)  15.9 us
    pallas_call x1, Pallas kernels, local(): pl.pallas_call(modes_kernel, out_shape=(jax.ShapeDtypeStruct((2, RANK, GR...  7.43 us
    pallas_call x1, Pallas kernels, local(): pl.pallas_call(focal_kernel, out_shape=(focal_shape, focal_shape, jax.Sha...  7.34 us
  transfers between devices with their start and end apart: 1, of which 0 were waited for; matrix products, arithmetic and copies ran while one was open for 0% of the time, Pallas kernels for 1%

profile of v1, /device:TPU:1, one launch (start us, length us, event | category | flops | bytes accessed | tf_op | source)
XLA Modules:
  0.0 122.1 jit_solution(9545108813399152819)
XLA Ops:
  0.6 16.6 %spectra.1 = bf16[128,4,16,128]{3,2,1,0:T(8,128)(2,1)} custom-call(s32[1]{0:T(128)} %bitcast.group_ref, s32[256]{0:T(256)} %assign_ref.1, f32[256]{0:T(256)} %occ_ref.1, f32[256]{0:T(256)} %chrom_ref.1, bf16[2,128,8,512]{3,2,1,0:T(8,128)(2,1)} %bitcast.7, f32[8,512]{1,0:T(8,128)} %lens_ref.1, bf16[512,512]{1,0:T(8,128)(2,1)} %constant.12.clone.cos_ref, ...), custom_call_target="tpu_custom_call" | custom-call | tf_op jit(solution)/shard_map/spectra/pallas_call | solution.py:253
  17.2 41.7 %all_to_all.15.pieces_ref = bf16[128,4,16,128]{3,2,1,0:T(8,128)(2,1)} all-to-all(bf16[128,4,16,128]{3,2,1,0:T(8,128)(2,1)} %spectra.1), channel_id=1, replica_groups=mesh['grp'=2,'pix'=64] {'grp','pix'}, dimensions={0} | all-to-all | bytes 4194304 | tf_op jit(solution)/shard_map/all_to_all | solution.py:266
  58.9 7.3 %focal.1 = (bf16[2,4,256,256]{3,2,1,0:T(8,128)(2,1)}, bf16[2,4,256,256]{3,2,1,0:T(8,128)(2,1)}, f32[512,128]{1,0:T(8,128)}) custom-call(s32[1]{0:T(128)} %bitcast.group_ref, bf16[128,4,16,128]{3,2,1,0:T(8,128)(2,1)} %all_to_all.15.pieces_ref, bf16[1024,1024]{1,0:T(8,128)(2,1)} %constant.14.clone.table_ref), custom_call_target="tpu_custom_call" | custom-call | tf_op jit(solution)/shard_map/focal/pallas_call | solution.py:268
  66.2 1.1 collective-permute-start
  67.4 28.7 %all_to_all.16 = f32[128,4,128]{2,1,0:T(4,128)} all-to-all(f32[128,4,128]{2,1,0:T(4,128)} %bitcast.11), channel_id=1, replica_groups=mesh['grp'=2,'pix'=64] {'grp','pix'}, dimensions={0} | all-to-all | bytes 524288 | tf_op jit(solution)/shard_map/all_to_all | solution.py:281
  96.1 1.7 %total.1 = f32[512,128]{1,0:T(8,128)} custom-call(f32[512,128]{1,0:T(8,128)} %bitcast.8), custom_call_target="tpu_custom_call" | custom-call | tf_op jit(solution)/shard_map/total/pallas_call | solution.py:282
  97.8 15.9 %all_to_all.17 = f32[128,4,128]{2,1,0:T(4,128)} all-to-all(f32[128,4,128]{2,1,0:T(4,128)} %bitcast.9), channel_id=1, replica_groups=mesh['grp'=2,'pix'=64] {'grp','pix'}, dimensions={0} | all-to-all | bytes 524288 | tf_op jit(solution)/shard_map/all_to_all | solution.py:290
  113.7 0.0 collective-permute-done.other_ref
  113.7 0.0 copy-start
  113.7 1.0 copy-done
  114.7 7.4 %modes.1 = (bf16[2,128,8,256]{3,2,1,0:T(8,128)(2,1)}, f32[1,128]{1,0:T(1,128)}) custom-call(s32[1]{0:T(128)} %bitcast.group_ref, f32[512,128]{1,0:T(8,128)} %bitcast.10, f32[2,256,128]{2,1,0:T(8,128)} %start_ref.1, bf16[2,4,256,256]{3,2,1,0:T(8,128)(2,1)} %get-tuple-element.8.keep_ref, bf16[2,4,256,256]{3,2,1,0:T(8,128)(2,1)} %copy-done), custom_call_target="tpu_custom_call" | custom-call | tf_op jit(solution)/shard_map/modes/pallas_call | solution.py:291
Async XLA Ops:
  66.2 47.5 %collective-permute-start = (bf16[2,4,256,256]{3,2,1,0:T(8,128)(2,1)}, bf16[2,4,256,256]{3,2,1,0:T(8,128)(2,1)S(1)}, u32[]{:S(2)}, u32[]{:S(2)}) collective-permute-start(bf16[2,4,256,256]{3,2,1,0:T(8,128)(2,1)} %get-tuple-element.9), channel_id=1, source_target_pairs={{0,64},{64,0},{1,65},{65,1},{2,66},{66,2},{3,67},{67,3},{4,68},{68... | collective-permute-start | bytes 3145736 | tf_op jit(solution)/shard_map/ppermute | solution.py:280
  113.7 1.0 copy-start

commit v2 on v1

--- a/solution.py
+++ b/solution.py
@@ -21,22 +21,22 @@
 COLS = NCOL // DEVICES
 HALF = NROW // GROUPS
 WIDE = RANK * GROUPS * COLS
+BLOCK = DEVICES * 2 * ROWS
 AXES = ("grp", "pix")
 
-PI_HI = 3.140625
-PI_LO = math.pi - 3.140625
+LIMIT = 0.5 * 1.5 * 3.140625
 
 
 def fit(function, terms):
-    limit = (math.pi / 2) * 1.001
+    limit = LIMIT * 1.001
     nodes = np.cos(np.pi * (np.arange(400) + 0.5) / 400)
     square = (nodes + 1.0) * 0.5 * limit * limit
     powers = np.stack([square**k for k in range(terms)], axis=1)
     return [float(c) for c in np.linalg.lstsq(powers, function(np.sqrt(square)), rcond=None)[0]]
 
 
-SIN_FIT = fit(lambda x: np.sin(x) / x, 5)
-COS_FIT = fit(np.cos, 6)
+SIN_FIT = fit(lambda x: np.sin(x) / x, 6)
+COS_FIT = fit(np.cos, 7)
 
 
 def tables(length):
@@ -82,54 +82,64 @@
     def phase(m, carry):
         electron = assign_ref[base + m]
         amplitude = jnp.sqrt(jnp.full((ROWS, 128), occ_ref[electron], jnp.float32))
-        chromatic = chrom_ref[electron]
+        twice = amplitude + amplitude
+        chromatic = chrom_ref[electron] * 0.5
         for lane in range(NCOL // 128):
             cut = pl.ds(lane * 128, 128)
-            angle = lens_ref[:, cut] * chromatic
-            turns = jnp.round(angle * (1.0 / math.pi))
-            rest = (angle - turns * PI_HI) - turns * PI_LO
-            square = rest * rest
-            signed = amplitude * (1.0 - 2.0 * (turns * turns))
-            sine = signed * (rest * polynomial(square, SIN_FIT))
-            cosine = signed * polynomial(square, COS_FIT)
+            half = lens_ref[:, cut] * chromatic
+            square = half * half
+            sine_half = half * polynomial(square, SIN_FIT)
+            scaled = sine_half * twice
+            sine = scaled * polynomial(square, COS_FIT)
+            cosine = amplitude - scaled * sine_half
             field_re = fields_ref[0, m, :, cut].astype(jnp.float32)
             field_im = fields_ref[1, m, :, cut].astype(jnp.float32)
-            rows = pl.ds(lane * ROWS * SLOTS + m, ROWS, stride=SLOTS)
+            rows = pl.ds(pl.multiple_of(lane * ROWS * SLOTS + m * ROWS, ROWS), ROWS)
             real_ref[rows, :] = field_re * cosine - field_im * sine
             imag_ref[rows, :] = field_re * sine + field_im * cosine
         return carry
 
-    lax.fori_loop(0, SLOTS, phase, 0, unroll=2)
+    lax.fori_loop(0, SLOTS, phase, 0, unroll=4)
     contract = (((1,), (1,)), ((), ()))
 
     def product(table, wave):
         return lax.dot_general(table, wave, contract, preferred_element_type=jnp.float32)
 
     def wave(ref, j):
-        lanes = [
-            ref[pl.ds((lane * ROWS + j) * SLOTS, 2 * SLOTS), :] for lane in range(NCOL // 128)
-        ]
-        return jnp.concatenate(lanes, axis=1).astype(jnp.bfloat16)
-
-    def spectrum(i, carry):
-        rows = pl.ds(pl.multiple_of(i * DEVICES, DEVICES), DEVICES)
-        cosine = cos_ref[rows, :]
-        sine = sin_ref[rows, :]
-        for j in range(0, ROWS, 2):
-            wave_re = wave(real_ref, j)
-            wave_im = wave(imag_ref, j)
-            across_re = product(cosine, wave_re) + product(sine, wave_im)
-            across_im = product(cosine, wave_im) - product(sine, wave_re)
-            for part, across in ((0, across_re), (1, across_im)):
-                for q in range(2):
-                    at = part * ROWS + j + q
+        return jnp.concatenate(
+            [
+                jnp.concatenate(
+                    [
+                        ref[pl.ds(lane * ROWS * SLOTS + j + q, SLOTS, stride=ROWS), :]
+                        for lane in range(NCOL // 128)
+                    ],
+                    axis=1,
+                )
+                for q in range(2)
+            ],
+            axis=0,
+        ).astype(jnp.bfloat16)
+
+    cosine = cos_ref[...]
+    sine = sin_ref[...]
+    for j in range(0, ROWS, 2):
+        wave_re = wave(real_ref, j)
+        wave_im = wave(imag_ref, j)
+        across_re = product(cosine, wave_re) + product(sine, wave_im)
+        across_im = product(cosine, wave_im) - product(sine, wave_re)
+        for part, across in ((0, across_re), (1, across_im)):
+            for q in range(2):
+                for i in range(COLS):
+                    at = i * BLOCK + part * ROWS + j + q
                     wide_ref[pl.ds(at, DEVICES, stride=2 * ROWS), :] = across[
-                        :, q * SLOTS : (q + 1) * SLOTS
+                        i * DEVICES : (i + 1) * DEVICES, q * SLOTS : (q + 1) * SLOTS
                     ]
-        out_ref[:, i] = wide_ref[...].astype(jnp.bfloat16).reshape(DEVICES, 2 * ROWS, SLOTS)
-        return carry
-
-    lax.fori_loop(0, COLS, spectrum, 0)
+    for i in range(COLS):
+        out_ref[:, i] = (
+            wide_ref[i * BLOCK : (i + 1) * BLOCK, :]
+            .astype(jnp.bfloat16)
+            .reshape(DEVICES, 2 * ROWS, SLOTS)
+        )
 
 
 def focal_kernel(group_ref, pieces_ref, table_ref, keep_ref, send_ref, gram_ref):
@@ -244,7 +254,10 @@
 
 VMEM = pl.BlockSpec(memory_space=pltpu.VMEM)
 SMEM = pl.BlockSpec(memory_space=pltpu.SMEM)
-PARAMS = pltpu.CompilerParams(vmem_limit_bytes=56 * 1024 * 1024)
+
+
+def params(mib):
+    return pltpu.CompilerParams(vmem_limit_bytes=mib * 1024 * 1024)
 
 
 def local(fields, lens_phase, occupancy, focus_scale, assignment, start_basis):
@@ -258,9 +271,9 @@
         scratch_shapes=[
             pltpu.VMEM((NCOL // 128 * ROWS * SLOTS, 128), jnp.float32),
             pltpu.VMEM((NCOL // 128 * ROWS * SLOTS, 128), jnp.float32),
-            pltpu.VMEM((DEVICES * 2 * ROWS, SLOTS), jnp.float32),
+            pltpu.VMEM((COLS * BLOCK, SLOTS), jnp.float32),
         ],
-        compiler_params=PARAMS,
+        compiler_params=params(20),
         name="spectra",
     )(group, assignment, occupancy, focus_scale, fields[0], lens_phase, cos_cols, sin_cols)
     pieces = lax.all_to_all(across, AXES, 0, 0, tiled=True)
@@ -274,7 +287,7 @@
         ),
         in_specs=[SMEM] + [VMEM] * 2,
         out_specs=(VMEM,) * 3,
-        compiler_params=PARAMS,
+        compiler_params=params(20),
         name="focal",
     )(group, pieces, jnp.asarray(row_tables()))
     other = lax.ppermute(send, "grp", [(0, 1), (1, 0)])
@@ -284,7 +297,7 @@
         out_shape=jax.ShapeDtypeStruct((4 * DEVICES, 128), jnp.float32),
         in_specs=[VMEM],
         out_specs=VMEM,
-        compiler_params=PARAMS,
+        compiler_params=params(4),
         name="total",
     )(parts.reshape(4 * DEVICES, 128))
     whole = lax.all_to_all(total.reshape(DEVICES, 4, 128), AXES, 0, 0, tiled=True)
@@ -297,7 +310,7 @@
         in_specs=[SMEM] + [VMEM] * 4,
         out_specs=(VMEM,) * 2,
         scratch_shapes=[pltpu.VMEM((HALF // 128 * WIDE, 128), jnp.float32)],
-        compiler_params=PARAMS,
+        compiler_params=params(20),
         name="modes",
     )(group, whole.reshape(4 * DEVICES, 128), start_basis, keep, other)
     return coherent_modes, power.reshape(RANK)

time: 122 us -> 110 us (0.902)
  Pallas kernels: 33.1 us -> 16.9 us
  local copies, waits for them, and re-layouts: 0.97 us -> 6.43 us
  blocking collectives: 86.3 us -> 84.8 us
    pallas_call x1, Pallas kernels: 16.6 us -> 7.11 us  [local(): pl.pallas_call(spectra_kernel, out_shape=jax.ShapeDtypeStruct((DEVICES, C...]
    unnamed x2 -> x18, local copies, waits for them, and re-layouts: 0.97 us -> 6.43 us
    pallas_call x1, Pallas kernels: 7.34 us -> 3.95 us  [local(): pl.pallas_call(focal_kernel, out_shape=(focal_shape, focal_shape, jax.Sha...]
    pallas_call x1, Pallas kernels: 7.43 us -> 5.77 us  [local(): pl.pallas_call(modes_kernel, out_shape=(jax.ShapeDtypeStruct((2, RANK, GR...]
    pallas_call x1, Pallas kernels: 1.73 us -> 0.09 us  [local(): pl.pallas_call(total_kernel, out_shape=jax.ShapeDtypeStruct((4 * DEVICES,...]
  transfers between devices with their start and end apart: 1 -> 1, of which waited for: 0 -> 0; matrix products, arithmetic and copies ran while one was open for 0% -> 0% of each run, Pallas kernels for 1% -> 0%
where the time goes in v2:
time: 110 us
  blocking collectives  84.8 us (77%)
  Pallas kernels  16.9 us (15%)
  local copies, waits for them, and re-layouts  6.43 us (6%)
  starting transfers between devices  1.21 us (1%)
    all_to_all x1, blocking collectives, local(): pieces = lax.all_to_all(across, AXES, 0, 0, tiled=True)  41.4 us
    all_to_all x1, blocking collectives, local(): lax.all_to_all(gram.reshape(DEVICES, 4, 128), AXES, 0, 0, tiled=True)  28.4 us
    all_to_all x1, blocking collectives, local(): lax.all_to_all(total.reshape(DEVICES, 4, 128), AXES, 0, 0, tiled=True)  15 us
    pallas_call x1, Pallas kernels, local(): pl.pallas_call(spectra_kernel, out_shape=jax.ShapeDtypeStruct((DEVICES, C...  7.11 us
    unnamed x18, local copies, waits for them, and re-layouts  6.43 us
    pallas_call x1, Pallas kernels, local(): pl.pallas_call(modes_kernel, out_shape=(jax.ShapeDtypeStruct((2, RANK, GR...  5.77 us
    pallas_call x1, Pallas kernels, local(): pl.pallas_call(focal_kernel, out_shape=(focal_shape, focal_shape, jax.Sha...  3.95 us
  transfers between devices with their start and end apart: 1, of which 0 were waited for; matrix products, arithmetic and copies ran while one was open for 0% of the time, Pallas kernels for 0%

profile of v2, /device:TPU:1, one launch (start us, length us, event | category | flops | bytes accessed | tf_op | source)
XLA Modules:
  0.0 110.0 jit_solution(4703777380161342372)
XLA Ops:
  0.6 0.0 copy-start
  0.6 1.6 %copy-done = bf16[1,2,128,8,512]{4,3,2,1,0:T(8,128)(2,1)S(1)} copy-done((bf16[1,2,128,8,512]{4,3,2,1,0:T(8,128)(2,1)S(1)}, bf16[1,2,128,8,512]{4,3,2,1,0:T(8,128)(2,1)}, u32[]{:S(2)}) %copy-start) | copy-done | bytes 2097176
  2.2 0.0 copy-start.2
  2.2 1.0 copy-done.2
  3.3 0.0 copy-start.3
  3.3 1.0 copy-done.3
  4.3 0.0 copy-start.5
  4.3 0.7 copy-done.5
  5.0 0.0 copy-start.6
  5.0 0.7 copy-done.6
  5.7 0.0 copy-start.7
  5.7 0.7 copy-done.7
  6.4 0.0 copy-start.8
  6.4 0.7 copy-done.8
  7.1 7.1 %spectra.1 = bf16[128,4,16,128]{3,2,1,0:T(8,128)(2,1)S(1)} custom-call(s32[1]{0:T(128)} %bitcast.group_ref, s32[256]{0:T(256)S(1)} %copy-done.6, f32[256]{0:T(256)S(1)} %copy-done.7, f32[256]{0:T(256)S(1)} %copy-done.8, bf16[2,128,8,512]{3,2,1,0:T(8,128)(2,1)S(1)} %bitcast.7, f32[8,512]{1,0:T(8,128)S(1)} %copy-done.5, bf16[512,512]{1,0:T(8,128)(2,1)S(1)} %copy-done.3, ...), custom_call_target="tpu_custom_call" | custom-call | tf_op jit(solution)/shard_map/spectra/pallas_call | solution.py:266
  14.2 0.0 copy-start.1
  14.2 41.4 %all_to_all.15.pieces_ref = bf16[128,4,16,128]{3,2,1,0:T(8,128)(2,1)S(1)} all-to-all(bf16[128,4,16,128]{3,2,1,0:T(8,128)(2,1)S(1)} %spectra.1), channel_id=1, replica_groups=mesh['grp'=2,'pix'=64] {'grp','pix'}, dimensions={0} | all-to-all | bytes 4194304 | tf_op jit(solution)/shard_map/all_to_all | solution.py:279
  55.6 0.0 copy-done.1
  55.6 0.0 copy-start.4
  55.6 3.9 %focal.1 = (bf16[2,4,256,256]{3,2,1,0:T(8,128)(2,1)S(1)}, bf16[2,4,256,256]{3,2,1,0:T(8,128)(2,1)S(1)}, f32[512,128]{1,0:T(8,128)S(1)}) custom-call(s32[1]{0:T(128)} %bitcast.group_ref, bf16[128,4,16,128]{3,2,1,0:T(8,128)(2,1)S(1)} %all_to_all.15.pieces_ref, bf16[1024,1024]{1,0:T(8,128)(2,1)S(1)} %copy-done.1), custom_call_target="tpu_custom_call" | custom-call | tf_op jit(solution)/shard_map/focal/pallas_call | solution.py:281
  59.5 1.2 %collective-permute-start = (bf16[2,4,256,256]{3,2,1,0:T(8,128)(2,1)S(1)}, bf16[2,4,256,256]{3,2,1,0:T(8,128)(2,1)S(1)}, u32[]{:S(2)}, u32[]{:S(2)}) collective-permute-start(bf16[2,4,256,256]{3,2,1,0:T(8,128)(2,1)S(1)} %get-tuple-element.9), channel_id=1, source_target_pairs={{0,64},{64,0},{1,65},{65,1},{2,66},{66,2},{3,67},{67,3},{4,68},{68... | collective-permute-start | bytes 3145736 | tf_op jit(solution)/shard_map/ppermute | solution.py:293
  60.8 28.4 %all_to_all.16 = f32[128,4,128]{2,1,0:T(4,128)S(1)} all-to-all(f32[128,4,128]{2,1,0:T(4,128)S(1)} %bitcast.11), channel_id=1, replica_groups=mesh['grp'=2,'pix'=64] {'grp','pix'}, dimensions={0} | all-to-all | bytes 524288 | tf_op jit(solution)/shard_map/all_to_all | solution.py:294
  89.2 0.1 total.1
  89.3 15.0 %all_to_all.17 = f32[128,4,128]{2,1,0:T(4,128)S(1)} all-to-all(f32[128,4,128]{2,1,0:T(4,128)S(1)} %bitcast.9), channel_id=1, replica_groups=mesh['grp'=2,'pix'=64] {'grp','pix'}, dimensions={0} | all-to-all | bytes 524288 | tf_op jit(solution)/shard_map/all_to_all | solution.py:303
  104.2 0.0 collective-permute-done.other_ref
  104.2 0.0 copy-done.4
  104.2 5.8 %modes.1 = (bf16[2,128,8,256]{3,2,1,0:T(8,128)(2,1)}, f32[1,128]{1,0:T(1,128)}) custom-call(s32[1]{0:T(128)} %bitcast.group_ref, f32[512,128]{1,0:T(8,128)S(1)} %bitcast.10, f32[2,256,128]{2,1,0:T(8,128)S(1)} %copy-done.4, bf16[2,4,256,256]{3,2,1,0:T(8,128)(2,1)S(1)} %get-tuple-element.8.keep_ref, bf16[2,4,256,256]{3,2,1,0:T(8,128)(2,1)S(1)} %collective-permute-done.other_ref), custom_call_target="tpu_custom_call" | custom-call | tf_op jit(solution)/shard_map/modes/pallas_call | solution.py:304
Async XLA Ops:
  0.6 1.6 %copy-start = (bf16[1,2,128,8,512]{4,3,2,1,0:T(8,128)(2,1)S(1)}, bf16[1,2,128,8,512]{4,3,2,1,0:T(8,128)(2,1)}, u32[]{:S(2)}) copy-start(bf16[1,2,128,8,512]{4,3,2,1,0:T(8,128)(2,1)} %param.9) | copy-start | bytes 6291460
  2.2 1.0 copy-start.2
  3.3 1.0 copy-start.3
  4.3 0.7 copy-start.5
  5.0 0.7 copy-start.6
  5.7 0.7 copy-start.7
  6.4 0.7 copy-start.8
  14.2 41.4 %copy-start.1 = (bf16[1024,1024]{1,0:T(8,128)(2,1)S(1)}, bf16[1024,1024]{1,0:T(8,128)(2,1)}, u32[]{:S(2)}) copy-start(bf16[1024,1024]{1,0:T(8,128)(2,1)} %constant.14.clone.table_ref) | copy-start | bytes 6291460
  55.6 48.6 %copy-start.4 = (f32[2,256,128]{2,1,0:T(8,128)S(1)}, f32[2,256,128]{2,1,0:T(8,128)}, u32[]{:S(2)}) copy-start(f32[2,256,128]{2,1,0:T(8,128)} %start_ref.1) | copy-start | bytes 786436
  59.5 44.7 %collective-permute-start = (bf16[2,4,256,256]{3,2,1,0:T(8,128)(2,1)S(1)}, bf16[2,4,256,256]{3,2,1,0:T(8,128)(2,1)S(1)}, u32[]{:S(2)}, u32[]{:S(2)}) collective-permute-start(bf16[2,4,256,256]{3,2,1,0:T(8,128)(2,1)S(1)} %get-tuple-element.9), channel_id=1, source_target_pairs={{0,64},{64,0},{1,65},{65,1},{2,66},{66,2},{3,67},{67,3},{4,68},{68... | collective-permute-start | bytes 3145736 | tf_op jit(solution)/shard_map/ppermute | solution.py:293

commit v3 on v2

--- a/solution.py
+++ b/solution.py
@@ -21,6 +21,9 @@
 COLS = NCOL // DEVICES
 HALF = NROW // GROUPS
 WIDE = RANK * GROUPS * COLS
+EARLY = 3
+CHUNKS = 4
+CHUNK = SLOTS // CHUNKS
 BLOCK = DEVICES * 2 * ROWS
 AXES = ("grp", "pix")
 
@@ -74,9 +77,40 @@
 
 
 def spectra_kernel(
-    group_ref, assign_ref, occ_ref, chrom_ref, fields_ref, lens_ref, cos_ref, sin_ref, out_ref,
-    real_ref, imag_ref, wide_ref,
+    group_ref, assign_hbm, occ_hbm, chrom_hbm, fields_hbm, lens_hbm, cos_hbm, sin_hbm, out_hbm,
+    assign_ref, occ_ref, chrom_ref, fields_ref, lens_ref, cos_ref, sin_ref,
+    real_ref, imag_ref, wide_ref, out_ref, small_sem, field_sem, table_sem, out_sem,
 ):
+    def chunk(part, c):
+        slots = pl.ds(c * CHUNK, CHUNK)
+        return pltpu.make_async_copy(
+            fields_hbm.at[part, slots], fields_ref.at[part, slots], field_sem.at[part, c]
+        )
+
+    small = [
+        pltpu.make_async_copy(source, target, small_sem.at[k])
+        for k, (source, target) in enumerate(
+            (
+                (assign_hbm, assign_ref),
+                (occ_hbm, occ_ref),
+                (chrom_hbm, chrom_ref),
+                (lens_hbm, lens_ref),
+            )
+        )
+    ]
+    large = [
+        pltpu.make_async_copy(cos_hbm, cos_ref, table_sem.at[0]),
+        pltpu.make_async_copy(sin_hbm, sin_ref, table_sem.at[1]),
+    ]
+    for copy in small:
+        copy.start()
+    for c in range(CHUNKS):
+        for part in range(2):
+            chunk(part, c).start()
+    for copy in large:
+        copy.start()
+    for copy in small:
+        copy.wait()
     base = group_ref[0] * SLOTS
 
     def phase(m, carry):
@@ -99,7 +133,12 @@
             imag_ref[rows, :] = field_re * sine + field_im * cosine
         return carry
 
-    lax.fori_loop(0, SLOTS, phase, 0, unroll=4)
+    for c in range(CHUNKS):
+        for part in range(2):
+            chunk(part, c).wait()
+        lax.fori_loop(c * CHUNK, (c + 1) * CHUNK, phase, 0, unroll=4)
+    for copy in large:
+        copy.wait()
     contract = (((1,), (1,)), ((), ()))
 
     def product(table, wave):
@@ -134,15 +173,20 @@
                     wide_ref[pl.ds(at, DEVICES, stride=2 * ROWS), :] = across[
                         i * DEVICES : (i + 1) * DEVICES, q * SLOTS : (q + 1) * SLOTS
                     ]
+    stores = []
     for i in range(COLS):
-        out_ref[:, i] = (
+        out_ref[i] = (
             wide_ref[i * BLOCK : (i + 1) * BLOCK, :]
             .astype(jnp.bfloat16)
             .reshape(DEVICES, 2 * ROWS, SLOTS)
         )
-
-
-def focal_kernel(group_ref, pieces_ref, table_ref, keep_ref, send_ref, gram_ref):
+        stores.append(pltpu.make_async_copy(out_ref.at[i], out_hbm.at[:, i], out_sem.at[i]))
+        stores[-1].start()
+    for copy in stores:
+        copy.wait()
+
+
+def focal_kernel(group_ref, pieces_ref, table_ref, keep_ref, early_ref, late_ref, gram_ref):
     group = group_ref[0]
     real = jnp.zeros((STACK, STACK), jnp.float32)
     cross = jnp.zeros((STACK, STACK), jnp.float32)
@@ -166,7 +210,11 @@
         for part in range(2):
             low, high = turned[part][:, :HALF], turned[part][:, HALF:]
             keep_ref[part, i] = jnp.where(group == 0, low, high)
-            send_ref[part, i] = jnp.where(group == 0, high, low)
+            sent = jnp.where(group == 0, high, low)
+            if i < EARLY:
+                early_ref[part, i] = sent
+            else:
+                late_ref[part, i - EARLY] = sent
         real += jnp.dot(turned[0], focal[0], preferred_element_type=jnp.float32)
         real += jnp.dot(turned[1], focal[1], preferred_element_type=jnp.float32)
         cross += jnp.dot(turned[0], focal[1], preferred_element_type=jnp.float32)
@@ -186,7 +234,7 @@
     out_ref[...] = jnp.broadcast_to(twice[None], (DEVICES // 2, 8, 128)).reshape(4 * DEVICES, 128)
 
 
-def modes_kernel(group_ref, gram_ref, start_ref, keep_ref, other_ref, out_ref, power_ref, wide_ref):
+def modes_kernel(group_ref, gram_ref, start_ref, keep_ref, early_ref, late_ref, out_ref, power_ref, wide_ref):
     highest = lax.Precision.HIGHEST
     quads = [gram_ref[pl.ds(q, 128, stride=4), :] for q in range(4)]
     packed = jnp.concatenate(
@@ -233,10 +281,13 @@
         return jnp.dot(a, b, preferred_element_type=jnp.float32)
 
     for part in range(2):
-        for source, ref in ((0, keep_ref), (1, other_ref)):
+        for source in range(2):
             first = jnp.where(group == source, 0, COLS)
             for i in range(COLS):
-                focal_re, focal_im = ref[0, i], ref[1, i]
+                ref, at = keep_ref, i
+                if source == 1:
+                    ref, at = (early_ref, i) if i < EARLY else (late_ref, i - EARLY)
+                focal_re, focal_im = ref[0, at], ref[1, at]
                 if part == 0:
                     mode = multiply(left_re, focal_re) - multiply(left_im, focal_im)
                 else:
@@ -253,6 +304,7 @@
 
 
 VMEM = pl.BlockSpec(memory_space=pltpu.VMEM)
+HBM = pl.BlockSpec(memory_space=pltpu.HBM)
 SMEM = pl.BlockSpec(memory_space=pltpu.SMEM)
 
 
@@ -266,31 +318,48 @@
     across = pl.pallas_call(
         spectra_kernel,
         out_shape=jax.ShapeDtypeStruct((DEVICES, COLS, 2 * ROWS, SLOTS), jnp.bfloat16),
-        in_specs=[SMEM] * 4 + [VMEM] * 4,
-        out_specs=VMEM,
+        in_specs=[SMEM] + [HBM] * 7,
+        out_specs=HBM,
         scratch_shapes=[
+            pltpu.SMEM((STACK,), jnp.int32),
+            pltpu.SMEM((STACK,), jnp.float32),
+            pltpu.SMEM((STACK,), jnp.float32),
+            pltpu.VMEM((2, SLOTS, ROWS, NCOL), jnp.bfloat16),
+            pltpu.VMEM((ROWS, NCOL), jnp.float32),
+            pltpu.VMEM((NCOL, NCOL), jnp.bfloat16),
+            pltpu.VMEM((NCOL, NCOL), jnp.bfloat16),
             pltpu.VMEM((NCOL // 128 * ROWS * SLOTS, 128), jnp.float32),
             pltpu.VMEM((NCOL // 128 * ROWS * SLOTS, 128), jnp.float32),
             pltpu.VMEM((COLS * BLOCK, SLOTS), jnp.float32),
+            pltpu.VMEM((COLS, DEVICES, 2 * ROWS, SLOTS), jnp.bfloat16),
+            pltpu.SemaphoreType.DMA((4,)),
+            pltpu.SemaphoreType.DMA((2, CHUNKS)),
+            pltpu.SemaphoreType.DMA((2,)),
+            pltpu.SemaphoreType.DMA((COLS,)),
         ],
-        compiler_params=params(20),
+        compiler_params=params(54),
         name="spectra",
     )(group, assignment, occupancy, focus_scale, fields[0], lens_phase, cos_cols, sin_cols)
     pieces = lax.all_to_all(across, AXES, 0, 0, tiled=True)
-    focal_shape = jax.ShapeDtypeStruct((2, COLS, STACK, HALF), jnp.bfloat16)
-    keep, send, gram = pl.pallas_call(
+
+    def focal_shape(count):
+        return jax.ShapeDtypeStruct((2, count, STACK, HALF), jnp.bfloat16)
+
+    keep, early, late, gram = pl.pallas_call(
         focal_kernel,
         out_shape=(
-            focal_shape,
-            focal_shape,
+            focal_shape(COLS),
+            focal_shape(EARLY),
+            focal_shape(COLS - EARLY),
             jax.ShapeDtypeStruct((4 * DEVICES, 128), jnp.float32),
         ),
         in_specs=[SMEM] + [VMEM] * 2,
-        out_specs=(VMEM,) * 3,
+        out_specs=(VMEM,) * 4,
         compiler_params=params(20),
         name="focal",
     )(group, pieces, jnp.asarray(row_tables()))
-    other = lax.ppermute(send, "grp", [(0, 1), (1, 0)])
+    early = lax.ppermute(early, "grp", [(0, 1), (1, 0)])
+    late = lax.ppermute(late, "grp", [(0, 1), (1, 0)])
     parts = lax.all_to_all(gram.reshape(DEVICES, 4, 128), AXES, 0, 0, tiled=True)
     total = pl.pallas_call(
         total_kernel,
@@ -307,16 +376,17 @@
             jax.ShapeDtypeStruct((2, RANK, GROUPS * COLS, HALF), jnp.bfloat16),
             jax.ShapeDtypeStruct((1, RANK), jnp.float32),
         ),
-        in_specs=[SMEM] + [VMEM] * 4,
+        in_specs=[SMEM] + [VMEM] * 5,
         out_specs=(VMEM,) * 2,
         scratch_shapes=[pltpu.VMEM((HALF // 128 * WIDE, 128), jnp.float32)],
         compiler_params=params(20),
         name="modes",
-    )(group, whole.reshape(4 * DEVICES, 128), start_basis, keep, other)
+    )(group, whole.reshape(4 * DEVICES, 128), start_basis, keep, early, late)
     return coherent_modes, power.reshape(RANK)
 
 
 def solution(mesh):
     in_specs = (P("grp", None, None, "pix", None), P("pix", None), P(), P(), P(), P())
     out_specs = (P(None, None, "pix", "grp"), P())
+
     return jax.shard_map(local, mesh=mesh, in_specs=in_specs, out_specs=out_specs, check_vma=False)

time: 110 us -> 104 us (0.945)
  blocking collectives: 84.8 us -> 41.6 us
  waiting for transfers between devices: 0.01 us -> 25.8 us
  starting transfers between devices: 1.21 us -> 14.8 us
  local copies, waits for them, and re-layouts: 6.43 us -> 0.72 us
  Pallas kernels: 16.9 us -> 20.2 us
    all_to_all x2 -> x0, blocking collectives: 43.4 us -> none  [the longest x1 28.4 us: local(): lax.all_to_all(gram.reshape(DEVICES, 4, 128), AXES, 0, 0, tiled=True)]
    all_to_all x0 -> x2, waiting for transfers between devices: none -> 25.8 us  [the longest x1 14.8 us: local(): lax.all_to_all(gram.reshape(DEVICES, 4, 128), AXES, 0, 0, tiled=True)]
    all_to_all x0 -> x2, starting transfers between devices: none -> 10.4 us  [the longest x1 6.1 us: local(): lax.all_to_all(gram.reshape(DEVICES, 4, 128), AXES, 0, 0, tiled=True)]
    unnamed x18 -> x6, local copies, waits for them, and re-layouts: 6.43 us -> 0.72 us
    ppermute x1 -> x2, starting transfers between devices: 1.21 us -> 4.47 us  [the longest x1 3.33 us: local(): late = lax.ppermute(late, 'grp', [(0, 1), (1, 0)])]
    pallas_call x1, Pallas kernels: 7.11 us -> 9.07 us  [local(): pl.pallas_call(spectra_kernel, out_shape=jax.ShapeDtypeStruct((DEVICES, C...]
  transfers between devices with their start and end apart: 1 -> 4, of which waited for: 0 -> 2; matrix products, arithmetic and copies ran while one was open for 0% -> 0% of each run, Pallas kernels for 0% -> 1%
where the time goes in v3:
time: 104 us
  blocking collectives  41.6 us (40%)
  waiting for transfers between devices  25.8 us (25%)
  Pallas kernels  20.2 us (19%)
  starting transfers between devices  14.8 us (14%)
    all_to_all x1, blocking collectives, local(): pieces = lax.all_to_all(across, AXES, 0, 0, tiled=True)  41.6 us
    all_to_all x1, waiting for transfers between devices, local(): lax.all_to_all(gram.reshape(DEVICES, 4, 128), AXES, 0, 0, tiled=True)  14.8 us
    all_to_all x1, waiting for transfers between devices, local(): lax.all_to_all(total.reshape(DEVICES, 4, 128), AXES, 0, 0, tiled=True)  11 us
    pallas_call x1, Pallas kernels, local(): pl.pallas_call(spectra_kernel, out_shape=jax.ShapeDtypeStruct((DEVICES, C...  9.07 us
    all_to_all x1, starting transfers between devices, local(): lax.all_to_all(gram.reshape(DEVICES, 4, 128), AXES, 0, 0, tiled=True)  6.1 us
    pallas_call x1, Pallas kernels, local(): pl.pallas_call(modes_kernel, out_shape=(jax.ShapeDtypeStruct((2, RANK, GR...  5.73 us
    pallas_call x1, Pallas kernels, local(): pl.pallas_call(focal_kernel, out_shape=(focal_shape(COLS), focal_shape(EA...  4.65 us
    all_to_all x1, starting transfers between devices, local(): lax.all_to_all(total.reshape(DEVICES, 4, 128), AXES, 0, 0, tiled=True)  4.27 us
  transfers between devices with their start and end apart: 4, of which 2 were waited for; matrix products, arithmetic and copies ran while one was open for 0% of the time, Pallas kernels for 1%

profile of v3, /device:TPU:1, one launch (start us, length us, event | category | flops | bytes accessed | tf_op | source)
XLA Modules:
  0.0 103.8 jit_solution(8676934635853763071)
XLA Ops:
  0.6 9.1 %spectra.1 = bf16[128,4,16,128]{3,2,1,0:T(8,128)(2,1)} custom-call(s32[1]{0:T(128)} %bitcast.group_ref, s32[256]{0:T(256)} %assign_hbm.1, f32[256]{0:T(256)} %occ_hbm.1, f32[256]{0:T(256)} %chrom_hbm.1, bf16[2,128,8,512]{3,2,1,0:T(8,128)(2,1)} %bitcast.9, f32[8,512]{1,0:T(8,128)} %lens_hbm.1, bf16[512,512]{1,0:T(8,128)(2,1)} %constant.12.clone.cos_hbm, ...), custom_call_target="tpu_custom_call" | custom-call | tf_op jit(solution)/shard_map/spectra/pallas_call | solution.py:318
  9.7 0.0 copy-start
  9.7 41.6 %all_to_all.15.pieces_ref = bf16[128,4,16,128]{3,2,1,0:T(8,128)(2,1)S(1)} all-to-all(bf16[128,4,16,128]{3,2,1,0:T(8,128)(2,1)} %spectra.1), channel_id=1, replica_groups=mesh['grp'=2,'pix'=64] {'grp','pix'}, dimensions={0} | all-to-all | bytes 4194304 | tf_op jit(solution)/shard_map/all_to_all | solution.py:343
  51.3 0.0 copy-done
  51.3 0.0 copy-start.1
  51.3 4.6 %focal.1 = (bf16[2,4,256,256]{3,2,1,0:T(8,128)(2,1)S(1)}, bf16[2,3,256,256]{3,2,1,0:T(8,128)(2,1)S(1)}, bf16[2,1,256,256]{3,2,1,0:T(8,128)(2,1)S(1)}, f32[512,128]{1,0:T(8,128)}) custom-call(s32[1]{0:T(128)} %bitcast.group_ref, bf16[128,4,16,128]{3,2,1,0:T(8,128)(2,1)S(1)} %all_to_all.15.pieces_ref, bf16[1024,1024]{1,0:T(8,128)(2,1)S(1)} %copy-done), custom_call_target="tpu_custom_call" | custom-call | tf_op jit(solution)/shard_map/focal/pallas_call | solution.py:348
  56.0 0.0 copy-start.2
  56.0 0.7 copy-done.2
  56.7 1.1 %collective-permute-start = (bf16[2,3,256,256]{3,2,1,0:T(8,128)(2,1)S(1)}, bf16[2,3,256,256]{3,2,1,0:T(8,128)(2,1)S(1)}, u32[]{:S(2)}, u32[]{:S(2)}) collective-permute-start(bf16[2,3,256,256]{3,2,1,0:T(8,128)(2,1)S(1)} %get-tuple-element.10), channel_id=1, source_target_pairs={{0,64},{64,0},{1,65},{65,1},{2,66},{66,2},{3,67},{67,3},{4,68},{68... | collective-permute-start | bytes 2359304 | tf_op jit(solution)/shard_map/ppermute | solution.py:361
  57.8 6.1 %all-to-all-start.1 = ((f32[128,4,128]{2,1,0:T(4,128)}), f32[128,4,128]{2,1,0:T(4,128)S(1)}, u32[]{:S(2)}, u32[]{:S(2)}) async-start(f32[128,4,128]{2,1,0:T(4,128)} %bitcast.2), calls=%async_computation.1 | async-start | bytes 524288 | tf_op jit(solution)/shard_map/all_to_all | solution.py:363
  63.9 3.3 %collective-permute-start.1 = (bf16[2,1,256,256]{3,2,1,0:T(8,128)(2,1)}, bf16[2,1,256,256]{3,2,1,0:T(8,128)(2,1)S(1)}, u32[]{:S(2)}, u32[]{:S(2)}) collective-permute-start(bf16[2,1,256,256]{3,2,1,0:T(8,128)(2,1)} %copy-done.2), channel_id=1, source_target_pairs={{0,64},{64,0},{1,65},{65,1},{2,66},{66,2},{3,67},{67,3},{4,68},{68... | collective-permute-start | bytes 786440 | tf_op jit(solution)/shard_map/ppermute | solution.py:362
  67.3 14.8 %all-to-all-done.1 = f32[128,4,128]{2,1,0:T(4,128)S(1)} async-done(((f32[128,4,128]{2,1,0:T(4,128)}), f32[128,4,128]{2,1,0:T(4,128)S(1)}, u32[]{:S(2)}, u32[]{:S(2)}) %all-to-all-start.1) | async-done | bytes 262176 | tf_op jit(solution)/shard_map/all_to_all | solution.py:363
  82.0 0.8 total.1
  82.8 4.3 %all-to-all-start.2 = ((f32[128,4,128]{2,1,0:T(4,128)}), f32[128,4,128]{2,1,0:T(4,128)S(1)}, u32[]{:S(2)}, u32[]{:S(2)}) async-start(f32[128,4,128]{2,1,0:T(4,128)} %bitcast.4), calls=%async_computation.2 | async-start | bytes 524288 | tf_op jit(solution)/shard_map/all_to_all | solution.py:372
  87.1 0.0 collective-permute-done.1.late_ref
  87.1 11.0 %all-to-all-done.2 = f32[128,4,128]{2,1,0:T(4,128)S(1)} async-done(((f32[128,4,128]{2,1,0:T(4,128)}), f32[128,4,128]{2,1,0:T(4,128)S(1)}, u32[]{:S(2)}, u32[]{:S(2)}) %all-to-all-start.2) | async-done | bytes 262176 | tf_op jit(solution)/shard_map/all_to_all | solution.py:372
  98.1 0.0 collective-permute-done.early_ref
  98.1 0.0 copy-done.1
  98.1 5.7 %modes.1 = (bf16[2,128,8,256]{3,2,1,0:T(8,128)(2,1)}, f32[1,128]{1,0:T(1,128)}) custom-call(s32[1]{0:T(128)} %bitcast.group_ref, f32[512,128]{1,0:T(8,128)S(1)} %bitcast.8, f32[2,256,128]{2,1,0:T(8,128)S(1)} %copy-done.1, bf16[2,4,256,256]{3,2,1,0:T(8,128)(2,1)S(1)} %get-tuple-element.9.keep_ref, ...), custom_call_target="tpu_custom_call" | custom-call | tf_op jit(solution)/shard_map/modes/pallas_call | solution.py:373
Async XLA Ops:
  9.7 41.6 %copy-start = (bf16[1024,1024]{1,0:T(8,128)(2,1)S(1)}, bf16[1024,1024]{1,0:T(8,128)(2,1)}, u32[]{:S(2)}) copy-start(bf16[1024,1024]{1,0:T(8,128)(2,1)} %constant.14.clone.table_ref) | copy-start | bytes 6291460
  51.3 46.8 %copy-start.1 = (f32[2,256,128]{2,1,0:T(8,128)S(1)}, f32[2,256,128]{2,1,0:T(8,128)}, u32[]{:S(2)}) copy-start(f32[2,256,128]{2,1,0:T(8,128)} %start_ref.1) | copy-start | bytes 786436
  56.0 0.7 copy-start.2
  56.7 41.4 %collective-permute-start = (bf16[2,3,256,256]{3,2,1,0:T(8,128)(2,1)S(1)}, bf16[2,3,256,256]{3,2,1,0:T(8,128)(2,1)S(1)}, u32[]{:S(2)}, u32[]{:S(2)}) collective-permute-start(bf16[2,3,256,256]{3,2,1,0:T(8,128)(2,1)S(1)} %get-tuple-element.10), channel_id=1, source_target_pairs={{0,64},{64,0},{1,65},{65,1},{2,66},{66,2},{3,67},{67,3},{4,68},{68... | collective-permute-start | bytes 2359304 | tf_op jit(solution)/shard_map/ppermute | solution.py:361
  57.8 24.2 %all-to-all-start.1 = ((f32[128,4,128]{2,1,0:T(4,128)}), f32[128,4,128]{2,1,0:T(4,128)S(1)}, u32[]{:S(2)}, u32[]{:S(2)}) async-start(f32[128,4,128]{2,1,0:T(4,128)} %bitcast.2), calls=%async_computation.1 | async-start | bytes 524288 | tf_op jit(solution)/shard_map/all_to_all | solution.py:363
  63.9 23.2 %collective-permute-start.1 = (bf16[2,1,256,256]{3,2,1,0:T(8,128)(2,1)}, bf16[2,1,256,256]{3,2,1,0:T(8,128)(2,1)S(1)}, u32[]{:S(2)}, u32[]{:S(2)}) collective-permute-start(bf16[2,1,256,256]{3,2,1,0:T(8,128)(2,1)} %copy-done.2), channel_id=1, source_target_pairs={{0,64},{64,0},{1,65},{65,1},{2,66},{66,2},{3,67},{67,3},{4,68},{68... | collective-permute-start | bytes 786440 | tf_op jit(solution)/shard_map/ppermute | solution.py:362
  82.8 15.3 %all-to-all-start.2 = ((f32[128,4,128]{2,1,0:T(4,128)}), f32[128,4,128]{2,1,0:T(4,128)S(1)}, u32[]{:S(2)}, u32[]{:S(2)}) async-start(f32[128,4,128]{2,1,0:T(4,128)} %bitcast.4), calls=%async_computation.2 | async-start | bytes 524288 | tf_op jit(solution)/shard_map/all_to_all | solution.py:372
